TPU v7x, 256 devices: a whole 4x4x8 slice. The times are simulated.
256 devices in a mesh: seq: 32 (over x, z), chan: 8 (over y, core).
Axes of the slice: x: 4, y: 4, z: 8, core: 2. Of those that a mesh axis runs over, the one named last changes fastest.
Arguments:
- query_rows: bfloat16 [8192, 2048], P('seq', 'chan'), may hold values from -6 to 6
- key_rows: bfloat16 [8192, 2048], P('seq', 'chan'), may hold values from -6 to 6
- value_rows: bfloat16 [8192, 2048], P('seq', 'chan'), may hold values from -6 to 6
- long_filter: float32 [8192, 2048], P('seq', 'chan'), may hold values from -2 to 2
- short_taps: float32 [3, 3, 2048], P(None, None, ('seq', 'chan')), may hold values from -3 to 3
- skip_gain: float32 [2048], P(('seq', 'chan')), may hold values from -3 to 3
- cotangent: bfloat16 [8192, 2048], P('seq', 'chan'), may hold values from -6 to 6
Outputs:
- gated_out: bfloat16 [8192, 2048], P('seq', 'chan')
- query_grad: bfloat16 [8192, 2048], P('seq', 'chan')
- key_grad: bfloat16 [8192, 2048], P('seq', 'chan')
- value_grad: bfloat16 [8192, 2048], P('seq', 'chan')
- filter_grad: float32 [8192, 2048], P('seq', 'chan')
- taps_grad: float32 [3, 3, 2048], P(None, None, 'chan')
- skip_grad: float32 [2048], P('chan')
All inputs are finite; a program needn't handle non-finite values.
Results may differ from a plain program's by a relative error of at most 0.00135.
Values may be sent and summed in bfloat16 or wider, within the bound.
A program may use at most 64 MiB of HBM per device.

v0:
```python
import math
import jax
import jax.numpy as jnp
from jax import lax
from jax.sharding import PartitionSpec as P

exact_dot = lax.Precision.HIGHEST


def from_behind(value, axis, by):
    length = lax.axis_size(axis)
    pairs = [(i, i + by) for i in range(length) if 0 <= i + by < length]
    return lax.ppermute(value, axis, pairs)


def angles(left_index, right_index, period):
    product = left_index[:, None] * right_index[None, :] % period
    return 2.0 * math.pi / period * product.astype(jnp.float32)


def source_transform(pieces, row_start, total):
    sources = pieces.shape[1]
    row_count = pieces.shape[2]
    source_index = jnp.arange(sources, dtype=jnp.int32)
    freq_index = jnp.arange(2 * sources, dtype=jnp.int32)
    theta = angles(source_index, freq_index, 2 * sources)
    real_part = jnp.einsum("fqrc,qk->fkrc", pieces, jnp.cos(theta), precision=exact_dot)
    imag_part = -jnp.einsum("fqrc,qk->fkrc", pieces, jnp.sin(theta), precision=exact_dot)
    row_index = row_start + jnp.arange(row_count, dtype=jnp.int32)
    twist = angles(freq_index, row_index, total)
    cosine = jnp.cos(twist)[None, :, :, None]
    sine = jnp.sin(twist)[None, :, :, None]
    return jnp.stack([real_part * cosine + imag_part * sine, imag_part * cosine - real_part * sine])


def row_transform(spectra, direction):
    length = spectra.shape[3]
    positions = jnp.arange(length, dtype=jnp.int32)
    theta = angles(positions, positions, length)
    cosine = jnp.cos(theta)
    sine = jnp.sin(theta)
    real_cos = jnp.einsum("femc,mk->fekc", spectra[0], cosine, precision=exact_dot)
    real_sin = jnp.einsum("femc,mk->fekc", spectra[0], sine, precision=exact_dot)
    imag_cos = jnp.einsum("femc,mk->fekc", spectra[1], cosine, precision=exact_dot)
    imag_sin = jnp.einsum("femc,mk->fekc", spectra[1], sine, precision=exact_dot)
    return jnp.stack([real_cos - direction * imag_sin, imag_cos + direction * real_sin])


def untwist(spectra, freq_start, total):
    freq_index = freq_start + jnp.arange(spectra.shape[2], dtype=jnp.int32)
    row_index = jnp.arange(spectra.shape[3], dtype=jnp.int32)
    twist = angles(freq_index, row_index, total)
    cosine = jnp.cos(twist)[None, :, :, None]
    sine = jnp.sin(twist)[None, :, :, None]
    return jnp.stack(
        [spectra[0] * cosine - spectra[1] * sine, spectra[1] * cosine + spectra[0] * sine]
    )


def source_sum(spectra, total):
    freqs = spectra.shape[2]
    theta = angles(
        jnp.arange(freqs // 2, dtype=jnp.int32), jnp.arange(freqs, dtype=jnp.int32), freqs
    )
    summed = jnp.einsum("fkrc,qk->fqrc", spectra[0], jnp.cos(theta), precision=exact_dot)
    summed = summed - jnp.einsum("fkrc,qk->fqrc", spectra[1], jnp.sin(theta), precision=exact_dot)
    return summed / total


def spectrum_split(fields):
    devices = lax.axis_size("seq")
    place = lax.axis_index("seq")
    nfields, row_count, channels = fields.shape
    share = row_count // devices
    total = 2 * devices * row_count
    mixed = source_transform(
        lax.all_to_all(
            fields.reshape(nfields, 1, row_count, channels),
            "seq",
            split_axis=2,
            concat_axis=1,
            tiled=True,
        ),
        place * share,
        total,
    )
    mixed = mixed.reshape(2, nfields, devices, 2, share, channels)
    return row_transform(
        lax.all_to_all(mixed, "seq", split_axis=2, concat_axis=4, tiled=True)[:, :, 0], -1.0
    )


def signal_split(spectra):
    devices = lax.axis_size("seq")
    place = lax.axis_index("seq")
    nfields = spectra.shape[1]
    row_count = spectra.shape[3]
    channels = spectra.shape[4]
    share = row_count // devices
    total = 2 * devices * row_count
    turned = untwist(row_transform(spectra, 1.0), 2 * place, total)
    turned = turned.reshape(2, nfields, 1, 2, devices, share, channels)
    pieces = lax.all_to_all(turned, "seq", split_axis=4, concat_axis=2, tiled=True)
    gathered = source_sum(pieces.reshape(2, nfields, 2 * devices, share, pieces.shape[6]), total)
    return lax.all_to_all(gathered, "seq", split_axis=1, concat_axis=2, tiled=True).reshape(
        nfields, row_count, channels
    )


def complex_product(left, right, conjugate):
    right_imag = -right[1] if conjugate else right[1]
    return jnp.stack(
        [left[0] * right[0] - left[1] * right_imag, left[0] * right_imag + left[1] * right[0]]
    )


def per_device(query_rows, key_rows, value_rows, long_filter, short_taps, skip_gain, cotangent):
    row_count, channels = query_rows.shape
    devices = lax.axis_size("seq")
    grad_scale = 1.0 / math.sqrt(row_count * devices)
    all_taps, all_gain = (
        lax.all_gather(short_taps, ("seq", "chan"), axis=2, tiled=True),
        lax.all_gather(skip_gain, ("seq", "chan"), axis=0, tiled=True),
    )
    start = lax.axis_index("chan") * channels
    tap_block = lax.dynamic_slice_in_dim(all_taps, start, channels, 2)
    skip_block = lax.dynamic_slice_in_dim(all_gain, start, channels, 0)
    streams = jnp.stack([query_rows, key_rows, value_rows])
    lower = from_behind(streams[:, row_count - 2 :, :], "seq", 1)
    extended = jnp.concatenate([lower, streams], axis=1).astype(jnp.float32)
    shorted = sum(
        (
            tap_block[:, offset, None, :] * extended[:, 2 - offset : 2 - offset + row_count]
            for offset in range(3)
        )
    )
    query_conv = shorted[0]
    key_conv = shorted[1]
    value_conv = shorted[2]
    product = key_conv * value_conv
    upstream = cotangent.astype(jnp.float32)
    gated_grad = upstream * query_conv
    spectra = spectrum_split(jnp.stack([product, long_filter]))
    prod_spec = spectra[:, 0]
    filt_spec = spectra[:, 1]
    conv_part = signal_split(complex_product(prod_spec, filt_spec, False)[:, None])[0]
    grad_spec = spectrum_split(gated_grad[None])[:, 0]
    back = signal_split(
        jnp.stack(
            [
                complex_product(grad_spec, filt_spec, True),
                complex_product(grad_spec, prod_spec, True),
            ],
            axis=1,
        )
    )
    corr_product = back[0]
    corr_filter = back[1]
    mixed_conv = conv_part + skip_block * product
    gated_out = (query_conv * mixed_conv).astype(jnp.bfloat16)
    query_conv_grad = upstream * mixed_conv
    product_grad = corr_product + skip_block * gated_grad
    filter_grad = grad_scale * corr_filter
    key_conv_grad = product_grad * value_conv
    value_conv_grad = product_grad * key_conv
    conv_grads = jnp.stack([query_conv_grad, key_conv_grad, value_conv_grad])
    upper = from_behind(conv_grads[:, :2, :], "seq", -1)
    ext_grads = jnp.concatenate([conv_grads, upper], axis=1)
    input_grads = sum(
        (
            tap_block[:, offset, None, :] * ext_grads[:, offset : offset + row_count]
            for offset in range(3)
        )
    ).astype(jnp.bfloat16)
    tap_terms = jnp.stack(
        [
            jnp.sum(conv_grads * extended[:, 2 - offset : 2 - offset + row_count], axis=1)
            for offset in range(3)
        ],
        axis=1,
    )
    skip_terms = jnp.sum(gated_grad * product, axis=0)
    tap_total, skip_total = lax.psum((tap_terms, skip_terms), "seq")
    return (
        gated_out,
        input_grads[0],
        input_grads[1],
        input_grads[2],
        filter_grad,
        grad_scale * tap_total,
        grad_scale * skip_total,
    )


def solution(mesh):
    in_specs = (
        P("seq", "chan"),
        P("seq", "chan"),
        P("seq", "chan"),
        P("seq", "chan"),
        P(None, None, ("seq", "chan")),
        P(("seq", "chan")),
        P("seq", "chan"),
    )
    out_specs = (
        P("seq", "chan"),
        P("seq", "chan"),
        P("seq", "chan"),
        P("seq", "chan"),
        P("seq", "chan"),
        P(None, None, "chan"),
        P("chan"),
    )
    return jax.shard_map(
        per_device, mesh=mesh, in_specs=in_specs, out_specs=out_specs, check_vma=False
    )
```

profile of v0, /device:TPU:8, one launch (start us, length us, event | category | flops | bytes accessed | tf_op | source)
XLA Modules:
  0.0 597.0 jit_solution(4957405621104877456)
XLA Ops:
  1.4 3.8 collective-permute-start
  6.0 83.8 %all_gather.6 = f32[3,3,2048]{1,0,2:T(4,128)} all-gather(f32[3,3,8]{1,0,2:T(4,128)S(1)} %copy.38), channel_id=1, replica_groups=mesh['seq'=32,'chan'=8] {'seq','chan'}, dimensions={2}, use_global_device_ids=true | all-gather | bytes 74016 | tf_op jit(solution)/shard_map/all_gather | solution.py:122
  89.7 2.1 constant_dynamic-slice_fusion.1
  94.4 7.2 %all-to-all-start.4 = ((f32[1,1,256,256]{3,1,0,2:T(1,128)}), f32[1,1,256,256]{3,1,0,2:T(1,128)S(1)}, u32[]{:S(2)}, u32[]{:S(2)}) async-start(f32[1,1,256,256]{3,1,0,2:T(1,128)} %copy.55), calls=%async_computation.4 | async-start | bytes 524288 | tf_op jit(solution)/shard_map/all_to_all | solution.py:77
  102.9 11.3 %all-to-all-done.4 = f32[1,1,256,256]{3,1,0,2:T(1,128)S(1)} async-done(((f32[1,1,256,256]{3,1,0,2:T(1,128)}), f32[1,1,256,256]{3,1,0,2:T(1,128)S(1)}, u32[]{:S(2)}, u32[]{:S(2)}) %all-to-all-start.4) | async-done | bytes 262176 | tf_op jit(solution)/shard_map/all_to_all | solution.py:77
  114.3 4.7 all-to-all-start
  123.4 12.5 %all-to-all-done = f32[2,1,256,256]{3,0,1,2:T(2,128)S(1)} async-done(((f32[2,1,256,256]{3,0,1,2:T(2,128)}), f32[2,1,256,256]{3,0,1,2:T(2,128)S(1)}, u32[]{:S(2)}, u32[]{:S(2)}) %all-to-all-start) | async-done | bytes 524320 | tf_op jit(solution)/shard_map/all_to_all | solution.py:77
  135.9 5.8 all-to-all-start.5
  147.4 2.7 pad_maximum_fusion
  150.1 2.5 copy.74
  152.7 17.1 %all-to-all-done.5 = f32[2,1,32,2,8,256]{5,3,4,1,0,2:T(2,128)} async-done(((f32[2,1,32,2,8,256]{5,3,4,1,0,2:T(2,128)}), f32[2,1,32,2,8,256]{5,3,4,1,0,2:T(2,128)}, u32[]{:S(2)}, u32[]{:S(2)}) %all-to-all-start.5) | async-done | bytes 1048608 | tf_op jit(solution)/shard_map/all_to_all | solution.py:89
  169.8 4.9 all-to-all-start.1
  174.8 2.4 fusion.254
  177.2 47.1 %all-to-all-done.1 = f32[2,2,32,2,8,256]{5,3,4,1,0,2:T(2,128)S(1)} async-done(((f32[2,2,32,2,8,256]{5,3,4,1,0,2:T(2,128)}), f32[2,2,32,2,8,256]{5,3,4,1,0,2:T(2,128)S(1)}, u32[]{:S(2)}, u32[]{:S(2)}) %all-to-all-start.1) | async-done | bytes 2097184 | tf_op jit(solution)/shard_map/all_to_all | solution.py:89
  225.2 2.0 fusion.23
  229.2 2.1 fusion.5
  231.3 2.1 fusion.3
  235.2 13.2 %fusion.49 = f32[256,2,256]{2,0,1:T(8,128)S(1)} fusion(f32[1,1,2,256,256]{4,3,2,1,0:T(8,128)S(1)} %get-tuple-element.40), kind=kOutput, calls=%fused_computation.91 | convolution fusion | flops 403570688 | bytes 1048576 | tf_op jit(solution)/shard_map/femc,mk->fekc/dot_general | solution.py:42
  253.1 6.2 %all-to-all-start.2 = ((f32[2,1,1,2,32,8,256]{6,5,3,2,1,0,4:T(8,128)}), f32[2,1,1,2,32,8,256]{6,5,3,2,1,0,4:T(8,128)}, u32[]{:S(2)}, u32[]{:S(2)}) async-start(f32[2,1,1,2,32,8,256]{6,5,3,2,1,0,4:T(8,128)} %copy.75), calls=%async_computation.2 | async-start | bytes 2097152 | tf_op jit(solution)/shard_map/all_to_all | solution.py:103
  260.9 2.7 fusion.11
  271.4 2.3 fusion
  273.7 2.3 subtract_bitcast_fusion
  277.8 9.7 %all-to-all-done.2 = f32[2,1,1,2,32,8,256]{6,5,3,2,1,0,4:T(8,128)} async-done(((f32[2,1,1,2,32,8,256]{6,5,3,2,1,0,4:T(8,128)}), f32[2,1,1,2,32,8,256]{6,5,3,2,1,0,4:T(8,128)}, u32[]{:S(2)}, u32[]{:S(2)}) %all-to-all-start.2) | async-done | bytes 1048608 | tf_op jit(solution)/shard_map/all_to_all | solution.py:103
  287.5 4.9 all-to-all-start.6
  295.7 46.4 %all-to-all-done.6 = f32[2,2,1,2,32,8,256]{6,5,3,1,2,0,4:T(8,128)S(1)} async-done(((f32[2,2,1,2,32,8,256]{6,5,3,1,2,0,4:T(8,128)}), f32[2,2,1,2,32,8,256]{6,5,3,1,2,0,4:T(8,128)S(1)}, u32[]{:S(2)}, u32[]{:S(2)}) %all-to-all-start.6) | async-done | bytes 2097184 | tf_op jit(solution)/shard_map/all_to_all | solution.py:103
  342.1 6.0 %all-to-all-start.3 = ((f32[1,32,8,256]{3,2,0,1:T(8,128)}), f32[1,32,8,256]{3,2,0,1:T(8,128)S(1)}, u32[]{:S(2)}, u32[]{:S(2)}) async-start(f32[1,32,8,256]{3,2,0,1:T(8,128)} %copy.54), calls=%async_computation.3 | async-start | bytes 524288 | tf_op jit(solution)/shard_map/all_to_all | solution.py:105
  352.7 2.7 copy.64
  355.4 2.9 squeeze.39
  362.2 9.8 %all-to-all-start.7 = ((f32[2,32,8,256]{3,2,0,1:T(8,128)}), f32[2,32,8,256]{3,2,0,1:T(8,128)S(1)}, u32[]{:S(2)}, u32[]{:S(2)}) async-start(f32[2,32,8,256]{3,2,0,1:T(8,128)} %copy.66), calls=%async_computation.7 | async-start | bytes 1048576 | tf_op jit(solution)/shard_map/all_to_all | solution.py:105
  372.3 75.6 %all-reduce = f32[2048]{0:T(1024)S(1)} all-reduce(f32[2048]{0:T(1024)S(1)} %dynamic-update-slice), channel_id=1, replica_groups=mesh['seq'=32,'chan'=8] {'seq','chan'}, use_global_device_ids=true, to_apply=%add | all-reduce | flops 2048 | bytes 16384
  450.8 3.5 collective-permute-done.1
  454.9 139.8 %all-reduce.1 = (f32[3,3,256]{2,0,1:T(4,128)S(1)}, f32[256]{0:T(256)S(1)}) all-reduce(f32[3,3,256]{2,0,1:T(4,128)S(1)} %pad_maximum_fusion.7, f32[256]{0:T(256)S(1)} %get-tuple-element.57), channel_id=1, replica_groups=mesh['seq'=32,'chan'=8] {'seq'}, use_global_device_ids=true, to_apply=%region_3.4 | all-reduce | flops 2560 | bytes 20480 | tf_op jit(solution)/shard_map/psum | solution.py:183
  (94 shorter events, 53.3 us)
Async XLA Ops:
  1.4 91.1 %collective-permute-start = (bf16[3,2,256]{2,1,0:T(2,128)(2,1)S(1)}, bf16[3,2,256]{2,1,0:T(2,128)(2,1)S(1)}, u32[]{:S(2)}, u32[]{:S(2)}) collective-permute-start(bf16[3,2,256]{2,1,0:T(2,128)(2,1)S(1)} %pad_maximum_fusion.8), channel_id=1, source_target_pairs={{0,8},{8,16},{16,24},{24,32},{32,40},{40,48},{48,56},{56,64},{64,7... | collective-permute-start | bytes 9224 | tf_op jit(solution)/shard_map/ppermute | solution.py:13
  89.7 2.7 copy-start.4
  89.7 2.7 copy-start.5
  89.7 2.8 copy-start.6
  92.5 0.9 copy-start.7
  92.6 9.1 %copy-start.9 = (f32[256,256]{1,0:T(8,128)S(1)}, f32[256,256]{1,0:T(8,128)}, u32[]{:S(2)}) copy-start(f32[256,256]{1,0:T(8,128)} %param.10) | copy-start | bytes 786436
  93.4 9.5 %copy-start = (f32[3,256,256]{2,1,0:T(8,128)}, f32[3,256,256]{2,1,0:T(8,128)S(1)}, u32[]{:S(2)}) copy-start(f32[3,256,256]{2,1,0:T(8,128)S(1)} %multiply_add_fusion) | copy-start | bytes 2359300
  94.4 19.9 %all-to-all-start.4 = ((f32[1,1,256,256]{3,1,0,2:T(1,128)}), f32[1,1,256,256]{3,1,0,2:T(1,128)S(1)}, u32[]{:S(2)}, u32[]{:S(2)}) async-start(f32[1,1,256,256]{3,1,0,2:T(1,128)} %copy.55), calls=%async_computation.4 | async-start | bytes 524288 | tf_op jit(solution)/shard_map/all_to_all | solution.py:77
  114.3 21.6 %all-to-all-start = ((f32[2,1,256,256]{3,0,1,2:T(2,128)}), f32[2,1,256,256]{3,0,1,2:T(2,128)S(1)}, u32[]{:S(2)}, u32[]{:S(2)}) async-start(f32[2,1,256,256]{3,0,1,2:T(2,128)} %copy.42), calls=%async_computation | async-start | bytes 1048576 | tf_op jit(solution)/shard_map/all_to_all | solution.py:77
  135.9 33.9 %all-to-all-start.5 = ((f32[2,1,32,2,8,256]{5,3,4,1,0,2:T(2,128)}), f32[2,1,32,2,8,256]{5,3,4,1,0,2:T(2,128)}, u32[]{:S(2)}, u32[]{:S(2)}) async-start(f32[2,1,32,2,8,256]{5,3,4,1,0,2:T(2,128)} %copy.78), calls=%async_computation.5 | async-start | bytes 2097152 | tf_op jit(solution)/shard_map/all_to_all | solution.py:89
  145.8 1.6 copy-start.2
  169.8 54.5 %all-to-all-start.1 = ((f32[2,2,32,2,8,256]{5,3,4,1,0,2:T(2,128)}), f32[2,2,32,2,8,256]{5,3,4,1,0,2:T(2,128)S(1)}, u32[]{:S(2)}, u32[]{:S(2)}) async-start(f32[2,2,32,2,8,256]{5,3,4,1,0,2:T(2,128)} %copy.74), calls=%async_computation.1 | async-start | bytes 4194304 | tf_op jit(solution)/shard_map/all_to_all | solution.py:89
  253.1 34.5 %all-to-all-start.2 = ((f32[2,1,1,2,32,8,256]{6,5,3,2,1,0,4:T(8,128)}), f32[2,1,1,2,32,8,256]{6,5,3,2,1,0,4:T(8,128)}, u32[]{:S(2)}, u32[]{:S(2)}) async-start(f32[2,1,1,2,32,8,256]{6,5,3,2,1,0,4:T(8,128)} %copy.75), calls=%async_computation.2 | async-start | bytes 2097152 | tf_op jit(solution)/shard_map/all_to_all | solution.py:103
  259.2 4.3 copy-start.3
  287.5 54.6 %all-to-all-start.6 = ((f32[2,2,1,2,32,8,256]{6,5,3,1,2,0,4:T(8,128)}), f32[2,2,1,2,32,8,256]{6,5,3,1,2,0,4:T(8,128)S(1)}, u32[]{:S(2)}, u32[]{:S(2)}) async-start(f32[2,2,1,2,32,8,256]{6,5,3,1,2,0,4:T(8,128)} %copy.79), calls=%async_computation.6 | async-start | bytes 4194304 | tf_op jit(solution)/shard_map/all_to_all | solution.py:103
  342.1 20.1 %all-to-all-start.3 = ((f32[1,32,8,256]{3,2,0,1:T(8,128)}), f32[1,32,8,256]{3,2,0,1:T(8,128)S(1)}, u32[]{:S(2)}, u32[]{:S(2)}) async-start(f32[1,32,8,256]{3,2,0,1:T(8,128)} %copy.54), calls=%async_computation.3 | async-start | bytes 524288 | tf_op jit(solution)/shard_map/all_to_all | solution.py:105
  360.3 11.7 %copy-start.10 = (f32[8]{0:T(128)S(1)}, f32[8]{0:T(128)}, u32[]{:S(2)}) copy-start(f32[8]{0:T(128)} %param.12) | copy-start | bytes 100
  360.3 87.6 %copy-start.1 = (f32[3,256,256]{2,1,0:T(8,128)S(1)}, f32[3,256,256]{2,1,0:T(8,128)}, u32[]{:S(2)}) copy-start(f32[3,256,256]{2,1,0:T(8,128)} %copy-done) | copy-start | bytes 2359300
  360.3 87.6 %copy-start.8 = (bf16[256,256]{1,0:T(8,128)(2,1)S(1)}, bf16[256,256]{1,0:T(8,128)(2,1)}, u32[]{:S(2)}) copy-start(bf16[256,256]{1,0:T(8,128)(2,1)} %param.13) | copy-start | bytes 393220
  362.2 85.8 %all-to-all-start.7 = ((f32[2,32,8,256]{3,2,0,1:T(8,128)}), f32[2,32,8,256]{3,2,0,1:T(8,128)S(1)}, u32[]{:S(2)}, u32[]{:S(2)}) async-start(f32[2,32,8,256]{3,2,0,1:T(8,128)} %copy.66), calls=%async_computation.7 | async-start | bytes 1048576 | tf_op jit(solution)/shard_map/all_to_all | solution.py:105
  448.8 5.5 collective-permute-start.1
where the time goes:
time: 606 us; the launch traced here: 597 us
  blocking collectives  299 us (49%)
  waiting for transfers between devices  148 us (24%)
  starting transfers between devices  54.5 us (9%)
  matrix products  50.8 us (8%)
  local copies, waits for them, and re-layouts  35.4 us (6%)
  other arithmetic  7.9 us (1%)
    psum x1, blocking collectives, per_device(): tap_total, skip_total = lax.psum((tap_terms, skip_terms), 'seq')  140 us
    all_gather x1, blocking collectives, per_device(): lax.all_gather(short_taps, ('seq', 'chan'), axis=2, tiled=True)  83.8 us
    unnamed x1, blocking collectives  75.6 us
    all_to_all x2, waiting for transfers between devices, spectrum_split(): lax.all_to_all(mixed, 'seq', split_axis=2, concat_axis=4, tiled=True)  64.2 us
    all_to_all x2, waiting for transfers between devices, signal_split(): lax.all_to_all(turned, 'seq', split_axis=4, concat_axis=2, tiled=True)  56.1 us
    all_to_all x2, waiting for transfers between devices, spectrum_split(): lax.all_to_all(fields.reshape(nfields, 1, row_count, channels), 'seq', sp...  23.8 us
    dot_general x4, matrix products, row_transform(): jnp.einsum('femc,mk->fekc', spectra[0], cosine, precision=exact_dot)  18.9 us
    all_to_all x2, starting transfers between devices, signal_split(): lax.all_to_all(gathered, 'seq', split_axis=1, concat_axis=2, tiled=True)  15.8 us
  transfers between devices with their start and end apart: 10, of which 7 were waited for; matrix products, arithmetic and copies ran while one was open for 10% of the time, Pallas kernels for 0%

commit v1 on v0

--- a/solution.py
+++ b/solution.py
@@ -3,6 +3,7 @@
 import jax.numpy as jnp
 from jax import lax
 from jax.sharding import PartitionSpec as P
+from jax.lax import all_to_all, psum
 
 exact_dot = lax.Precision.HIGHEST
 
@@ -118,8 +119,16 @@
     row_count, channels = query_rows.shape
     devices = lax.axis_size("seq")
     grad_scale = 1.0 / math.sqrt(row_count * devices)
+
+    def unite_the_column(m):
+        all_values = all_to_all(
+            jnp.stack(psum(1, ("seq", "chan")) * [m]), ("seq", "chan"), concat_axis=0, split_axis=0
+        )
+        reached = jnp.concatenate(all_values, axis=2)
+        return reached
+
     all_taps, all_gain = (
-        lax.all_gather(short_taps, ("seq", "chan"), axis=2, tiled=True),
+        unite_the_column(short_taps),
         lax.all_gather(skip_gain, ("seq", "chan"), axis=0, tiled=True),
     )
     start = lax.axis_index("chan") * channels

time: 606 us -> 562 us (0.927)
  blocking collectives: 299 us -> 214 us
  waiting for transfers between devices: 148 us -> 176 us
  starting transfers between devices: 54.5 us -> 64.6 us
    all_gather x1 -> x0, blocking collectives: 83.8 us -> none  [per_device(): lax.all_gather(short_taps, ('seq', 'chan'), axis=2, tiled=True)]
    ppermute x2, waiting for transfers between devices: 3.5 us -> 29.1 us  [from_behind(): return lax.ppermute(value, axis, pairs)]
    all_to_all x0 -> x1, starting transfers between devices: none -> 14.6 us  [unite_the_column(): all_to_all(jnp.stack(psum(1, ('seq', 'chan')) * [m]), ('seq', 'chan'), co...]
    dot_general x4, matrix products: 7.3 us -> 21 us  [row_transform(): jnp.einsum('femc,mk->fekc', spectra[1], cosine, precision=exact_dot)]
    all_to_all x0 -> x1, waiting for transfers between devices: none -> 13.2 us  [unite_the_column(): all_to_all(jnp.stack(psum(1, ('seq', 'chan')) * [m]), ('seq', 'chan'), co...]
    dot_general x4, matrix products: 18.9 us -> 8.14 us  [row_transform(): jnp.einsum('femc,mk->fekc', spectra[0], cosine, precision=exact_dot)]
  transfers between devices with their start and end apart: 10 -> 11, of which waited for: 7 -> 9; matrix products, arithmetic and copies ran while one was open for 10% -> 11% of each run, Pallas kernels for 0% -> 0%
where the time goes in v1:
time: 562 us; the launch traced here: 555 us
  blocking collectives  214 us (38%)
  waiting for transfers between devices  176 us (31%)
  starting transfers between devices  64.6 us (11%)
  matrix products  53.8 us (10%)
  local copies, waits for them, and re-layouts  36.8 us (7%)
  other arithmetic  7.29 us (1%)
    psum x1, blocking collectives, per_device(): tap_total, skip_total = lax.psum((tap_terms, skip_terms), 'seq')  139 us
    unnamed x1, blocking collectives  74.7 us
    all_to_all x2, waiting for transfers between devices, spectrum_split(): lax.all_to_all(mixed, 'seq', split_axis=2, concat_axis=4, tiled=True)  58.9 us
    all_to_all x2, waiting for transfers between devices, signal_split(): lax.all_to_all(turned, 'seq', split_axis=4, concat_axis=2, tiled=True)  52.3 us
    ppermute x2, waiting for transfers between devices, from_behind(): return lax.ppermute(value, axis, pairs)  29.1 us
    all_to_all x2, waiting for transfers between devices, spectrum_split(): lax.all_to_all(fields.reshape(nfields, 1, row_count, channels), 'seq', sp...  22.7 us
    dot_general x4, matrix products, row_transform(): jnp.einsum('femc,mk->fekc', spectra[1], cosine, precision=exact_dot)  21 us
    all_to_all x2, starting transfers between devices, signal_split(): lax.all_to_all(gathered, 'seq', split_axis=1, concat_axis=2, tiled=True)  15.2 us
  transfers between devices with their start and end apart: 11, of which 9 were waited for; matrix products, arithmetic and copies ran while one was open for 11% of the time, Pallas kernels for 0%

profile of v1, /device:TPU:8, one launch (start us, length us, event | category | flops | bytes accessed | tf_op | source)
XLA Modules:
  0.0 554.5 jit_solution(1014714905160768524)
XLA Ops:
  0.7 2.1 stack.68
  2.8 14.6 %all-to-all-start = ((f32[256,3,3,8]{3,2,1,0:T(4,128)}), f32[256,3,3,8]{3,2,1,0:T(4,128)S(1)}, u32[]{:S(2)}, u32[]{:S(2)}) async-start(f32[256,3,3,8]{3,2,1,0:T(4,128)} %stack.68), calls=%async_computation | async-start | bytes 3145728 | tf_op jit(solution)/shard_map/all_to_all | solution.py:124
  17.5 3.6 collective-permute-start
  21.0 25.6 %collective-permute-done = bf16[3,2,256]{2,1,0:T(2,128)(2,1)S(1)} collective-permute-done((bf16[3,2,256]{2,1,0:T(2,128)(2,1)S(1)}, bf16[3,2,256]{2,1,0:T(2,128)(2,1)S(1)}, u32[]{:S(2)}, u32[]{:S(2)}) %collective-permute-start) | collective-permute-done | bytes 3104 | tf_op jit(solution)/shard_map/ppermute | solution.py:14
  46.7 13.2 %all-to-all-done = f32[256,3,3,8]{3,2,1,0:T(4,128)S(1)} async-done(((f32[256,3,3,8]{3,2,1,0:T(4,128)}), f32[256,3,3,8]{3,2,1,0:T(4,128)S(1)}, u32[]{:S(2)}, u32[]{:S(2)}) %all-to-all-start) | async-done | bytes 73760 | tf_op jit(solution)/shard_map/all_to_all | solution.py:124
  64.4 3.9 all-to-all-start.5
  69.7 11.0 %all-to-all-done.5 = f32[1,1,256,256]{3,1,0,2:T(1,128)S(1)} async-done(((f32[1,1,256,256]{3,1,0,2:T(1,128)}), f32[1,1,256,256]{3,1,0,2:T(1,128)S(1)}, u32[]{:S(2)}, u32[]{:S(2)}) %all-to-all-start.5) | async-done | bytes 262176 | tf_op jit(solution)/shard_map/all_to_all | solution.py:78
  80.7 4.4 all-to-all-start.1
  89.5 11.7 %all-to-all-done.1 = f32[2,1,256,256]{3,0,1,2:T(2,128)S(1)} async-done(((f32[2,1,256,256]{3,0,1,2:T(2,128)}), f32[2,1,256,256]{3,0,1,2:T(2,128)S(1)}, u32[]{:S(2)}, u32[]{:S(2)}) %all-to-all-start.1) | async-done | bytes 524320 | tf_op jit(solution)/shard_map/all_to_all | solution.py:78
  101.2 5.6 %all-to-all-start.6 = ((f32[2,1,32,2,8,256]{5,3,4,1,0,2:T(2,128)}), f32[2,1,32,2,8,256]{5,3,4,1,0,2:T(2,128)}, u32[]{:S(2)}, u32[]{:S(2)}) async-start(f32[2,1,32,2,8,256]{5,3,4,1,0,2:T(2,128)} %copy.76), calls=%async_computation.6 | async-start | bytes 2097152 | tf_op jit(solution)/shard_map/all_to_all | solution.py:90
  112.6 2.7 pad_maximum_fusion
  115.4 2.6 copy.72
  117.9 16.0 %all-to-all-done.6 = f32[2,1,32,2,8,256]{5,3,4,1,0,2:T(2,128)} async-done(((f32[2,1,32,2,8,256]{5,3,4,1,0,2:T(2,128)}), f32[2,1,32,2,8,256]{5,3,4,1,0,2:T(2,128)}, u32[]{:S(2)}, u32[]{:S(2)}) %all-to-all-start.6) | async-done | bytes 1048608 | tf_op jit(solution)/shard_map/all_to_all | solution.py:90
  133.9 5.4 all-to-all-start.2
  139.4 2.4 fusion.254
  141.8 2.5 fusion.40
  144.2 43.0 %all-to-all-done.2 = f32[2,2,32,2,8,256]{5,3,4,1,0,2:T(2,128)S(1)} async-done(((f32[2,2,32,2,8,256]{5,3,4,1,0,2:T(2,128)}), f32[2,2,32,2,8,256]{5,3,4,1,0,2:T(2,128)S(1)}, u32[]{:S(2)}, u32[]{:S(2)}) %all-to-all-start.2) | async-done | bytes 2097184 | tf_op jit(solution)/shard_map/all_to_all | solution.py:90
  196.4 14.3 %fusion.45 = f32[256,2,256]{2,0,1:T(8,128)S(1)} fusion(f32[1,1,2,256,256]{4,3,2,1,0:T(8,128)S(1)} %get-tuple-element.36), kind=kOutput, calls=%fused_computation.87 | convolution fusion | flops 403570688 | bytes 1048576 | tf_op jit(solution)/shard_map/femc,mk->fekc/dot_general | solution.py:45
  217.0 5.6 %all-to-all-start.3 = ((f32[2,1,1,2,32,8,256]{6,5,3,2,1,0,4:T(8,128)}), f32[2,1,1,2,32,8,256]{6,5,3,2,1,0,4:T(8,128)}, u32[]{:S(2)}, u32[]{:S(2)}) async-start(f32[2,1,1,2,32,8,256]{6,5,3,2,1,0,4:T(8,128)} %copy.73), calls=%async_computation.3 | async-start | bytes 2097152 | tf_op jit(solution)/shard_map/all_to_all | solution.py:104
  222.6 2.8 fusion.11
  225.4 2.7 fusion.36
  236.4 2.5 subtract_bitcast_fusion
  240.8 8.0 %all-to-all-done.3 = f32[2,1,1,2,32,8,256]{6,5,3,2,1,0,4:T(8,128)} async-done(((f32[2,1,1,2,32,8,256]{6,5,3,2,1,0,4:T(8,128)}), f32[2,1,1,2,32,8,256]{6,5,3,2,1,0,4:T(8,128)}, u32[]{:S(2)}, u32[]{:S(2)}) %all-to-all-start.3) | async-done | bytes 1048608 | tf_op jit(solution)/shard_map/all_to_all | solution.py:104
  248.8 5.1 all-to-all-start.7
  257.1 44.3 %all-to-all-done.7 = f32[2,2,1,2,32,8,256]{6,5,3,1,2,0,4:T(8,128)S(1)} async-done(((f32[2,2,1,2,32,8,256]{6,5,3,1,2,0,4:T(8,128)}), f32[2,2,1,2,32,8,256]{6,5,3,1,2,0,4:T(8,128)S(1)}, u32[]{:S(2)}, u32[]{:S(2)}) %all-to-all-start.7) | async-done | bytes 2097184 | tf_op jit(solution)/shard_map/all_to_all | solution.py:104
  301.5 5.4 all-to-all-start.4
  311.5 2.7 copy.62
  314.2 2.9 squeeze.39
  321.0 9.8 %all-to-all-start.8 = ((f32[2,32,8,256]{3,2,0,1:T(8,128)}), f32[2,32,8,256]{3,2,0,1:T(8,128)S(1)}, u32[]{:S(2)}, u32[]{:S(2)}) async-start(f32[2,32,8,256]{3,2,0,1:T(8,128)} %copy.64), calls=%async_computation.8 | async-start | bytes 1048576 | tf_op jit(solution)/shard_map/all_to_all | solution.py:106
  331.1 74.7 %all-reduce = f32[2048]{0:T(1024)S(1)} all-reduce(f32[2048]{0:T(1024)S(1)} %dynamic-update-slice), channel_id=1, replica_groups=mesh['seq'=32,'chan'=8] {'seq','chan'}, use_global_device_ids=true, to_apply=%add | all-reduce | flops 2048 | bytes 16384
  408.8 3.5 collective-permute-done.1
  412.9 139.3 %all-reduce.1 = (f32[3,3,256]{2,0,1:T(4,128)S(1)}, f32[256]{0:T(256)S(1)}) all-reduce(f32[3,3,256]{2,0,1:T(4,128)S(1)} %pad_maximum_fusion.7, f32[256]{0:T(256)S(1)} %get-tuple-element.54), channel_id=1, replica_groups=mesh['seq'=32,'chan'=8] {'seq'}, use_global_device_ids=true, to_apply=%region_3.4 | all-reduce | flops 2560 | bytes 20480 | tf_op jit(solution)/shard_map/psum | solution.py:192
  (95 shorter events, 59.0 us)
Async XLA Ops:
  0.6 16.8 %copy-start.3 = (bf16[256,256]{1,0:T(8,128)(2,1)S(1)}, bf16[256,256]{1,0:T(8,128)(2,1)}, u32[]{:S(2)}) copy-start(bf16[256,256]{1,0:T(8,128)(2,1)} %param.9) | copy-start | bytes 393220
  0.6 16.8 %copy-start.4 = (bf16[256,256]{1,0:T(8,128)(2,1)S(1)}, bf16[256,256]{1,0:T(8,128)(2,1)}, u32[]{:S(2)}) copy-start(bf16[256,256]{1,0:T(8,128)(2,1)} %param.8) | copy-start | bytes 393220
  0.7 16.8 %copy-start.5 = (bf16[256,256]{1,0:T(8,128)(2,1)S(1)}, bf16[256,256]{1,0:T(8,128)(2,1)}, u32[]{:S(2)}) copy-start(bf16[256,256]{1,0:T(8,128)(2,1)} %param.7) | copy-start | bytes 393220
  2.8 57.1 %all-to-all-start = ((f32[256,3,3,8]{3,2,1,0:T(4,128)}), f32[256,3,3,8]{3,2,1,0:T(4,128)S(1)}, u32[]{:S(2)}, u32[]{:S(2)}) async-start(f32[256,3,3,8]{3,2,1,0:T(4,128)} %stack.68), calls=%async_computation | async-start | bytes 3145728 | tf_op jit(solution)/shard_map/all_to_all | solution.py:124
  17.5 29.2 %collective-permute-start = (bf16[3,2,256]{2,1,0:T(2,128)(2,1)S(1)}, bf16[3,2,256]{2,1,0:T(2,128)(2,1)S(1)}, u32[]{:S(2)}, u32[]{:S(2)}) collective-permute-start(bf16[3,2,256]{2,1,0:T(2,128)(2,1)S(1)} %pad_maximum_fusion.8), channel_id=1, source_target_pairs={{0,8},{8,16},{16,24},{24,32},{32,40},{40,48},{48,56},{56,64},{64,7... | collective-permute-start | bytes 9224 | tf_op jit(solution)/shard_map/ppermute | solution.py:14
  61.0 2.3 copy-start.6
  63.1 5.3 copy-start.8
  63.4 6.3 %copy-start = (f32[3,256,256]{2,1,0:T(8,128)}, f32[3,256,256]{2,1,0:T(8,128)S(1)}, u32[]{:S(2)}) copy-start(f32[3,256,256]{2,1,0:T(8,128)S(1)} %multiply_add_fusion) | copy-start | bytes 2359300
  64.4 16.3 %all-to-all-start.5 = ((f32[1,1,256,256]{3,1,0,2:T(1,128)}), f32[1,1,256,256]{3,1,0,2:T(1,128)S(1)}, u32[]{:S(2)}, u32[]{:S(2)}) async-start(f32[1,1,256,256]{3,1,0,2:T(1,128)} %copy.53), calls=%async_computation.5 | async-start | bytes 524288 | tf_op jit(solution)/shard_map/all_to_all | solution.py:78
  80.7 20.6 %all-to-all-start.1 = ((f32[2,1,256,256]{3,0,1,2:T(2,128)}), f32[2,1,256,256]{3,0,1,2:T(2,128)S(1)}, u32[]{:S(2)}, u32[]{:S(2)}) async-start(f32[2,1,256,256]{3,0,1,2:T(2,128)} %copy.40), calls=%async_computation.1 | async-start | bytes 1048576 | tf_op jit(solution)/shard_map/all_to_all | solution.py:78
  101.2 32.7 %all-to-all-start.6 = ((f32[2,1,32,2,8,256]{5,3,4,1,0,2:T(2,128)}), f32[2,1,32,2,8,256]{5,3,4,1,0,2:T(2,128)}, u32[]{:S(2)}, u32[]{:S(2)}) async-start(f32[2,1,32,2,8,256]{5,3,4,1,0,2:T(2,128)} %copy.76), calls=%async_computation.6 | async-start | bytes 2097152 | tf_op jit(solution)/shard_map/all_to_all | solution.py:90
  111.0 1.6 copy-start.2
  133.9 53.3 %all-to-all-start.2 = ((f32[2,2,32,2,8,256]{5,3,4,1,0,2:T(2,128)}), f32[2,2,32,2,8,256]{5,3,4,1,0,2:T(2,128)S(1)}, u32[]{:S(2)}, u32[]{:S(2)}) async-start(f32[2,2,32,2,8,256]{5,3,4,1,0,2:T(2,128)} %copy.72), calls=%async_computation.2 | async-start | bytes 4194304 | tf_op jit(solution)/shard_map/all_to_all | solution.py:90
  217.0 31.8 %all-to-all-start.3 = ((f32[2,1,1,2,32,8,256]{6,5,3,2,1,0,4:T(8,128)}), f32[2,1,1,2,32,8,256]{6,5,3,2,1,0,4:T(8,128)}, u32[]{:S(2)}, u32[]{:S(2)}) async-start(f32[2,1,1,2,32,8,256]{6,5,3,2,1,0,4:T(8,128)} %copy.73), calls=%async_computation.3 | async-start | bytes 2097152 | tf_op jit(solution)/shard_map/all_to_all | solution.py:104
  248.8 52.7 %all-to-all-start.7 = ((f32[2,2,1,2,32,8,256]{6,5,3,1,2,0,4:T(8,128)}), f32[2,2,1,2,32,8,256]{6,5,3,1,2,0,4:T(8,128)S(1)}, u32[]{:S(2)}, u32[]{:S(2)}) async-start(f32[2,2,1,2,32,8,256]{6,5,3,1,2,0,4:T(8,128)} %copy.77), calls=%async_computation.7 | async-start | bytes 4194304 | tf_op jit(solution)/shard_map/all_to_all | solution.py:104
  301.5 19.5 %all-to-all-start.4 = ((f32[1,32,8,256]{3,2,0,1:T(8,128)}), f32[1,32,8,256]{3,2,0,1:T(8,128)S(1)}, u32[]{:S(2)}, u32[]{:S(2)}) async-start(f32[1,32,8,256]{3,2,0,1:T(8,128)} %copy.52), calls=%async_computation.4 | async-start | bytes 524288 | tf_op jit(solution)/shard_map/all_to_all | solution.py:106
  319.1 11.7 %copy-start.9 = (f32[8]{0:T(128)S(1)}, f32[8]{0:T(128)}, u32[]{:S(2)}) copy-start(f32[8]{0:T(128)} %param.12) | copy-start | bytes 100
  319.1 86.8 %copy-start.1 = (f32[3,256,256]{2,1,0:T(8,128)S(1)}, f32[3,256,256]{2,1,0:T(8,128)}, u32[]{:S(2)}) copy-start(f32[3,256,256]{2,1,0:T(8,128)} %copy-done) | copy-start | bytes 2359300
  319.1 86.8 %copy-start.7 = (bf16[256,256]{1,0:T(8,128)(2,1)S(1)}, bf16[256,256]{1,0:T(8,128)(2,1)}, u32[]{:S(2)}) copy-start(bf16[256,256]{1,0:T(8,128)(2,1)} %param.13) | copy-start | bytes 393220
  321.0 84.9 %all-to-all-start.8 = ((f32[2,32,8,256]{3,2,0,1:T(8,128)}), f32[2,32,8,256]{3,2,0,1:T(8,128)S(1)}, u32[]{:S(2)}, u32[]{:S(2)}) async-start(f32[2,32,8,256]{3,2,0,1:T(8,128)} %copy.64), calls=%async_computation.8 | async-start | bytes 1048576 | tf_op jit(solution)/shard_map/all_to_all | solution.py:106
  406.8 5.5 collective-permute-start.1
